TPU v7x, 256 devices: a whole 4x4x8 slice. The times are simulated.
256 devices in a mesh: gz: 32 (over x, z_hi, core), ord: 8 (over y, z_lo).
Axes of the slice: x: 4, y: 4, z: 8 (z_hi: 4, z_lo: 2; z = z_hi * 2 + z_lo), core: 2. Of those that a mesh axis runs over, the one named last changes fastest.
Arguments:
- initial: float32 [96, 64, 128, 128], P('ord', 'gz'), may hold values from -1 to 1
- cotangent: float32 [96, 64, 128, 128], P('ord', 'gz'), may hold values from -6 to 6
- mobility: float32 [96], P('ord'), may hold values from 0.05 to 0.15
- stiffness: float32 [96], P('ord'), may hold values from 0.5 to 1
Outputs:
- adjoint_initial: float32 [96, 64, 128, 128], P('ord', 'gz')
All inputs are finite; a program needn't handle non-finite values.
Results may differ from a plain program's by a relative error of at most 0.00002.
Values sent between devices are 32-bit elements; how exact they have to be, the bound alone decides.
A program may use at most 128 MiB of HBM per device.

v0:
```python
import jax
import jax.numpy as jnp
from jax import lax
from jax.sharding import PartitionSpec as P

P_SIZE = 96
couple_scale = 2.0


def extended(block, sides, width):
    for axis, dim in sides:
        count = lax.axis_size(axis)
        forward = [(i, i + 1) for i in range(count - 1)]
        forward.append((count - 1, 0))
        backward = [(target, source) for source, target in forward]
        low = lax.ppermute(
            lax.slice_in_dim(block, block.shape[dim] - width, None, axis=dim), axis, forward
        )
        high = lax.ppermute(lax.slice_in_dim(block, 0, width, axis=dim), axis, backward)
        block = jnp.concatenate([low, block, high], axis=dim)
    return block


def inner_laplacian(values_ext):
    centre = values_ext[:, 1:-1]
    summed = values_ext[:, 2:] + values_ext[:, :-2] - 6.0 * centre
    for axis_num in (2, 3):
        summed = summed + jnp.roll(centre, 1, axis_num) + jnp.roll(centre, -1, axis_num)
    return summed


def well_slope(values, squares, coupling):
    return (
        -1.0 + 3.0 * values * values + 2.0 * coupling * squares - 6.0 * coupling * values * values
    )


def on_device(initial, cotangent, mobility, stiffness):
    order_dev = initial.shape[0]
    coupling = couple_scale / P_SIZE
    rate_col = mobility.reshape(-1, 1, 1, 1)
    stiff_col = stiffness.reshape(-1, 1, 1, 1)
    margin = 1
    joined = extended(jnp.concatenate((initial, cotangent), 0), (("gz", 1),), margin)
    field_ext = joined[:order_dev]
    adjoint_ext = joined[order_dev:]
    centre = field_ext[:, 1:-1]
    squares_first = lax.psum(jnp.sum(centre * centre, 0), "ord")
    potential = (
        -centre
        + centre * centre * centre
        + 2.0 * coupling * centre * (squares_first - centre * centre)
        - stiff_col * inner_laplacian(field_ext)
    )
    middle = centre - rate_col * potential
    scaled_ext = rate_col * adjoint_ext
    scaled = scaled_ext[:, 1:-1]
    squares_second, coupled_second = lax.psum(
        (jnp.sum(middle * middle, 0), jnp.sum(middle * scaled, 0)), "ord"
    )
    adjoint_middle = adjoint_ext[:, 1:-1] - (
        well_slope(middle, squares_second, coupling) * scaled
        + 4.0 * coupling * middle * coupled_second
        - stiff_col * inner_laplacian(scaled_ext)
    )
    scaled_middle = rate_col * adjoint_middle
    scaled_middle_ext = extended(scaled_middle, (("gz", 1),), 1)
    scaled_inner = scaled_middle_ext[:, 1:-1]
    coupled_first = lax.psum(jnp.sum(initial * scaled_inner, 0), "ord")
    return adjoint_middle - (
        well_slope(initial, squares_first, coupling) * scaled_inner
        + 4.0 * coupling * initial * coupled_first
        - stiff_col * inner_laplacian(scaled_middle_ext)
    )


def solution(mesh):
    return jax.shard_map(
        on_device,
        mesh=mesh,
        in_specs=(P("ord", "gz", None, None), P("ord", "gz", None, None), P("ord"), P("ord")),
        out_specs=P("ord", "gz", None, None),
        check_vma=False,
    )
```

profile of v0, /device:TPU:2, one launch (start us, length us, event | category | flops | bytes accessed | tf_op | source)
XLA Modules:
  0.0 316.3 jit_solution(2872398733217685041)
XLA Ops:
  6.5 2.4 multiply_reduce_fusion
  9.1 1.9 fusion.47
  11.8 5.7 %collective-permute-start = (f32[24,1,128,128]{3,2,1,0:T(8,128)}, f32[24,1,128,128]{3,2,1,0:T(8,128)S(1)}, u32[]{:S(2)}, u32[]{:S(2)}) collective-permute-start(f32[24,1,128,128]{3,2,1,0:T(8,128)} %get-tuple-element.22), channel_id=1, source_target_pairs={{8,0},{16,8},{24,16},{32,24},{40,32},{48,40},{56,48},{64,56},{72,6... | collective-permute-start | bytes 4718600 | tf_op jit(solution)/shard_map/ppermute | solution.py:19
  17.6 2.0 fusion.54
  19.5 2.2 fusion.55
  21.7 2.3 fusion.56
  24.0 86.5 %all-reduce.5.cloned.1.call-done = f32[2,128,128]{2,1,0:T(8,128)} async-done(((f32[2,128,128]{2,1,0:T(8,128)}), f32[2,128,128]{2,1,0:T(8,128)}) %all-reduce.5.cloned.1.call-update) | async-done | bytes 131088 | tf_op jit(solution)/shard_map/psum | solution.py:48
  111.5 2.1 fusion
  113.6 2.0 fusion.44
  115.5 2.2 fusion.45
  118.3 1.0 copy-done.9
  119.7 1.1 copy-done.3
  121.6 4.8 %multiply_reduce_fusion.3 = (f32[2,128,128]{2,1,0:T(8,128)}, f32[2,128,128]{2,1,0:T(8,128)}, f32[12,2,128,128]{3,2,1,0:T(8,128)}) fusion(f32[12,4,128,128]{3,2,1,0:T(8,128)S(1)} %fusion, f32[12,2,128,128]{3,2,1,0:T(8,128)S(1)} %copy-done, f32[12,2,128,1]{3,2,1,0:T(8,128)S(1)} %copy-done.8, f32[12,2,128,127]{3,2,1,0:T(8,128)S(1)} %copy-done.10, ...), kind=kLoop, calls=%fused_computation.57 | loop fusion | flops 11337728 | bytes 17694816 | tf_op jit(solution)/shard_map/reduce_sum | solution.py:59
  126.5 4.3 %fusion.46 = (f32[12,2,128,127]{3,2,1,0:T(8,128)}, f32[12,2,128,127]{3,2,1,0:T(8,128)}) fusion(f32[12,4,128,128]{3,2,1,0:T(8,128)} %copy-done.1), kind=kLoop, calls=%fused_computation.68 | loop fusion | bytes 6242304 | tf_op jit(solution)/shard_map/jit(_roll_static)/slice | solution.py:28
  130.8 1.0 fusion.43
  131.8 72.7 %all-reduce.9.cloned.1.call-done = (f32[2,128,128]{2,1,0:T(8,128)}, f32[2,128,128]{2,1,0:T(8,128)}) async-done(((f32[2,128,128]{2,1,0:T(8,128)}, f32[2,128,128]{2,1,0:T(8,128)}), (f32[2,128,128]{2,1,0:T(8,128)}, f32[2,128,128]{2,1,0:T(8,128)})) %all-reduce.9.cloned.1.call-update) | async-done | bytes 262160 | tf_op jit(solution)/shard_map/psum | solution.py:58
  204.5 1.0 broadcast_multiply_fusion.2
  205.5 8.8 %multiply_reduce_fusion.1 = (f32[2,128,128]{2,1,0:T(8,128)}, f32[12,2,128,128]{3,2,1,0:T(8,128)S(1)}, f32[12,2,128,128]{3,2,1,0:T(8,128)}) fusion(f32[12,2,128,128]{3,2,1,0:T(8,128)S(1)} %copy-done, f32[12]{0:T(128)S(1)} %copy-done.12, f32[12,2,128,128]{3,2,1,0:T(8,128)} %param.5, f32[12,2,128,1]{3,2,1,0:T(8,128)} %get-tuple-element.18, ...), kind=kLoop, calls=%fused_computation.55 | loop fusion | flops 10584064 | bytes 19267680 | tf_op jit(solution)/shard_map/reduce_sum | solution.py:69
  214.3 2.2 fusion.48
  216.5 2.2 fusion.49
  218.7 1.3 fusion.52
  220.6 2.1 fusion.50
  222.7 79.8 %all-reduce.7.cloned.1.call-done = f32[2,128,128]{2,1,0:T(8,128)} async-done(((f32[2,128,128]{2,1,0:T(8,128)}), f32[2,128,128]{2,1,0:T(8,128)}) %all-reduce.7.cloned.1.call-update) | async-done | bytes 131088 | tf_op jit(solution)/shard_map/psum | solution.py:69
  303.4 6.4 %fusion.20 = f32[12,2,128,128]{3,2,1,0:T(8,128)} fusion(f32[12,2,128,128]{3,2,1,0:T(8,128)} %get-tuple-element.11, f32[12,2,128,128]{3,2,1,0:T(8,128)S(1)} %get-tuple-element.10, f32[12,2,128,128]{3,2,1,0:T(8,128)S(1)} %copy-done, f32[12,1,128,128]{3,2,1,0:T(8,128)} %collective-permute-done.3, f32[12,1,128,128]{3,2,1,0:T(8,128)} %collective-permute-done.2, ...), kind=kLoop, calls=%fused_computation.29 | loop fusion | flops 10223616 | bytes 14417968 | tf_op jit(solution)/shard_map/sub | solution.py:70
  (44 shorter events, 5.3 us)
Async XLA Ops:
  6.5 2.4 copy-start.4
  6.5 104.0 %all-reduce.5.cloned.1.call-start = ((), (), s32[]{:S(2)}) async-start(), calls=%async_computation | async-start | bytes 262144 | tf_op jit(solution)/shard_map/psum | solution.py:48
  9.1 2.7 copy-start.2
  9.1 8.4 %copy-start = (f32[12,2,128,128]{3,2,1,0:T(8,128)S(1)}, f32[12,2,128,128]{3,2,1,0:T(8,128)}, u32[]{:S(2)}) copy-start(f32[12,2,128,128]{3,2,1,0:T(8,128)} %param.4) | copy-start | bytes 4718596
  11.8 99.7 %collective-permute-start = (f32[24,1,128,128]{3,2,1,0:T(8,128)}, f32[24,1,128,128]{3,2,1,0:T(8,128)S(1)}, u32[]{:S(2)}, u32[]{:S(2)}) collective-permute-start(f32[24,1,128,128]{3,2,1,0:T(8,128)} %get-tuple-element.22), channel_id=1, source_target_pairs={{8,0},{16,8},{24,16},{32,24},{40,32},{48,40},{56,48},{64,56},{72,6... | collective-permute-start | bytes 4718600 | tf_op jit(solution)/shard_map/ppermute | solution.py:19
  17.5 94.0 %collective-permute-start.1 = (f32[24,1,128,128]{3,2,1,0:T(8,128)}, f32[24,1,128,128]{3,2,1,0:T(8,128)}, u32[]{:S(2)}, u32[]{:S(2)}) collective-permute-start(f32[24,1,128,128]{3,2,1,0:T(8,128)} %get-tuple-element.21), channel_id=1, source_target_pairs={{0,8},{8,16},{16,24},{24,32},{32,40},{40,48},{48,56},{56,64},{64,7... | collective-permute-start | bytes 4718600 | tf_op jit(solution)/shard_map/ppermute | solution.py:16
  17.5 187.0 %all-reduce.9.cloned.1.call-start = ((), (), s32[]{:S(2)}) async-start(), calls=%async_computation.2 | async-start | bytes 524288 | tf_op jit(solution)/shard_map/psum | solution.py:58
  21.7 89.7 %copy-start.12 = (f32[12]{0:T(128)S(1)}, f32[12]{0:T(128)}, u32[]{:S(2)}) copy-start(f32[12]{0:T(128)} %param.6) | copy-start | bytes 148
  111.4 6.8 %copy-start.11 = (f32[2,128,128]{2,1,0:T(8,128)S(1)}, f32[2,128,128]{2,1,0:T(8,128)}, u32[]{:S(2)}) copy-start(f32[2,128,128]{2,1,0:T(8,128)} %all-reduce.5.cloned.1.call-done) | copy-start | bytes 393220
  113.5 4.7 %copy-start.1 = (f32[12,4,128,128]{3,2,1,0:T(8,128)}, f32[12,4,128,128]{3,2,1,0:T(8,128)S(1)}, u32[]{:S(2)}) copy-start(f32[12,4,128,128]{3,2,1,0:T(8,128)S(1)} %fusion) | copy-start | bytes 9437188
  113.5 4.7 %copy-start.7 = (f32[12,2,128,1]{3,2,1,0:T(8,128)S(1)}, f32[12,2,128,1]{3,2,1,0:T(8,128)}, u32[]{:S(2)}) copy-start(f32[12,2,128,1]{3,2,1,0:T(8,128)} %get-tuple-element.39) | copy-start | bytes 36868
  113.5 4.7 %copy-start.8 = (f32[12,2,128,1]{3,2,1,0:T(8,128)S(1)}, f32[12,2,128,1]{3,2,1,0:T(8,128)}, u32[]{:S(2)}) copy-start(f32[12,2,128,1]{3,2,1,0:T(8,128)} %get-tuple-element.40) | copy-start | bytes 36868
  113.5 5.7 %copy-start.9 = (f32[12,2,128,127]{3,2,1,0:T(8,128)S(1)}, f32[12,2,128,127]{3,2,1,0:T(8,128)}, u32[]{:S(2)}) copy-start(f32[12,2,128,127]{3,2,1,0:T(8,128)} %get-tuple-element.41) | copy-start | bytes 4681732
  113.6 6.2 %copy-start.10 = (f32[12,2,128,127]{3,2,1,0:T(8,128)S(1)}, f32[12,2,128,127]{3,2,1,0:T(8,128)}, u32[]{:S(2)}) copy-start(f32[12,2,128,127]{3,2,1,0:T(8,128)} %get-tuple-element.42) | copy-start | bytes 4681732
  115.5 5.2 %copy-start.3 = (f32[24,2,128,128]{3,2,1,0:T(8,128)S(1)}, f32[24,2,128,128]{3,2,1,0:T(8,128)}, u32[]{:S(2)}) copy-start(f32[24,2,128,128]{3,2,1,0:T(8,128)} %copy-done.2) | copy-start | bytes 9437188
  115.5 5.7 %copy-start.5 = (f32[12,2,127,128]{3,2,1,0:T(8,128)S(1)}, f32[12,2,127,128]{3,2,1,0:T(8,128)}, u32[]{:S(2)}) copy-start(f32[12,2,127,128]{3,2,1,0:T(8,128)} %get-tuple-element.37) | copy-start | bytes 4681732
  115.5 6.1 %copy-start.6 = (f32[12,2,127,128]{3,2,1,0:T(8,128)S(1)}, f32[12,2,127,128]{3,2,1,0:T(8,128)}, u32[]{:S(2)}) copy-start(f32[12,2,127,128]{3,2,1,0:T(8,128)} %get-tuple-element.38) | copy-start | bytes 4681732
  115.5 6.1 %copy-start.13 = (f32[12]{0:T(128)S(1)}, f32[12]{0:T(128)}, u32[]{:S(2)}) copy-start(f32[12]{0:T(128)} %param.7) | copy-start | bytes 148
  126.5 176.0 %all-reduce.7.cloned.1.call-start = ((), (), s32[]{:S(2)}) async-start(), calls=%async_computation.1 | async-start | bytes 262144 | tf_op jit(solution)/shard_map/psum | solution.py:69
  220.0 83.3 %collective-permute-start.2 = (f32[12,1,128,128]{3,2,1,0:T(8,128)}, f32[12,1,128,128]{3,2,1,0:T(8,128)}, u32[]{:S(2)}, u32[]{:S(2)}) collective-permute-start(f32[12,1,128,128]{3,2,1,0:T(8,128)} %get-tuple-element.31), channel_id=1, source_target_pairs={{8,0},{16,8},{24,16},{32,24},{40,32},{48,40},{56,48},{64,56},{72,6... | collective-permute-start | bytes 2359304 | tf_op jit(solution)/shard_map/ppermute | solution.py:19
  220.0 83.4 %collective-permute-start.3 = (f32[12,1,128,128]{3,2,1,0:T(8,128)}, f32[12,1,128,128]{3,2,1,0:T(8,128)}, u32[]{:S(2)}, u32[]{:S(2)}) collective-permute-start(f32[12,1,128,128]{3,2,1,0:T(8,128)} %get-tuple-element.32), channel_id=1, source_target_pairs={{0,8},{8,16},{16,24},{24,32},{32,40},{40,48},{48,56},{56,64},{64,7... | collective-permute-start | bytes 2359304 | tf_op jit(solution)/shard_map/ppermute | solution.py:16
Sparse Core Ops, SparseCore 0:
  17.6 92.8 all-reduce.4
  126.6 77.8 all-reduce.8
  220.7 81.7 all-reduce.6
where the time goes:
time: 317 us; the launch traced here: 316 us
  waiting for transfers between devices  239 us (75%)
  local copies, waits for them, and re-layouts  30.3 us (10%)
  other arithmetic  27.4 us (9%)
  between operations  13.3 us (4%)
  starting transfers between devices  6.31 us (2%)
    psum x1, waiting for transfers between devices, on_device(): squares_first = lax.psum(jnp.sum(centre * centre, 0), 'ord')  86.5 us
    psum x1, waiting for transfers between devices, on_device(): coupled_first = lax.psum(jnp.sum(initial * scaled_inner, 0), 'ord')  79.8 us
    psum x1, waiting for transfers between devices, on_device(): lax.psum((jnp.sum(middle * middle, 0), jnp.sum(middle * scaled, 0)), 'ord')  72.7 us
    slice x8, local copies, waits for them, and re-layouts, inner_laplacian(): jnp.roll(centre, 1, axis_num)  15.9 us
    reduce_sum x1, other arithmetic, on_device(): coupled_first = lax.psum(jnp.sum(initial * scaled_inner, 0), 'ord')  8.83 us
    slice x4, local copies, waits for them, and re-layouts, inner_laplacian(): jnp.roll(centre, -1, axis_num)  6.48 us
    sub x1, other arithmetic, on_device(): adjoint_middle - (well_slope(initial, squares_first, coupling) * scaled_i...  6.4 us
  transfers between devices with their start and end apart: 7, of which 3 were waited for; matrix products, arithmetic and copies ran while one was open for 5% of the time, Pallas kernels for 0%

commit v1 on v0

--- a/solution.py
+++ b/solution.py
@@ -45,7 +45,7 @@
     field_ext = joined[:order_dev]
     adjoint_ext = joined[order_dev:]
     centre = field_ext[:, 1:-1]
-    squares_first = lax.psum(jnp.sum(centre * centre, 0), "ord")
+    squares_first = jnp.sum(lax.all_gather(jnp.sum(centre * centre, 0), "ord"), axis=0)
     potential = (
         -centre
         + centre * centre * centre

time: 317 us -> 278 us (0.88)
  waiting for transfers between devices: 239 us -> 203 us
  local copies, waits for them, and re-layouts: 30.3 us -> 24.9 us
    psum x1 -> x0, waiting for transfers between devices: 86.5 us -> none  [on_device(): squares_first = lax.psum(jnp.sum(centre * centre, 0), 'ord')]
    ppermute x2, waiting for transfers between devices: 0.01 us -> 23.9 us  [extended(): lax.ppermute(lax.slice_in_dim(block, block.shape[dim] - width, None, axis...]
    ppermute x2, waiting for transfers between devices: 0.01 us -> 20.9 us  [extended(): lax.ppermute(lax.slice_in_dim(block, 0, width, axis=dim), axis, backward)]
    psum x1, waiting for transfers between devices: 72.7 us -> 78.7 us  [on_device(): lax.psum((jnp.sum(middle * middle, 0), jnp.sum(middle * scaled, 0)), 'ord')]
    unnamed x28 -> x14, local copies, waits for them, and re-layouts: 4.65 us -> 0.79 us
  transfers between devices with their start and end apart: 7 -> 7, of which waited for: 3 -> 4; matrix products, arithmetic and copies ran while one was open for 5% -> 7% of each run, Pallas kernels for 0% -> 0%
where the time goes in v1:
time: 278 us
  waiting for transfers between devices  203 us (73%)
  other arithmetic  30 us (11%)
  local copies, waits for them, and re-layouts  24.9 us (9%)
  between operations  13.2 us (5%)
  starting transfers between devices  6.31 us (2%)
    psum x1, waiting for transfers between devices, on_device(): coupled_first = lax.psum(jnp.sum(initial * scaled_inner, 0), 'ord')  79.8 us
    psum x1, waiting for transfers between devices, on_device(): lax.psum((jnp.sum(middle * middle, 0), jnp.sum(middle * scaled, 0)), 'ord')  78.7 us
    ppermute x2, waiting for transfers between devices, extended(): lax.ppermute(lax.slice_in_dim(block, block.shape[dim] - width, None, axis...  23.9 us
    ppermute x2, waiting for transfers between devices, extended(): lax.ppermute(lax.slice_in_dim(block, 0, width, axis=dim), axis, backward)  20.9 us
    slice x8, local copies, waits for them, and re-layouts, inner_laplacian(): jnp.roll(centre, 1, axis_num)  14.3 us
    reduce_sum x1, other arithmetic, on_device(): coupled_first = lax.psum(jnp.sum(initial * scaled_inner, 0), 'ord')  8.83 us
    reduce_sum x1, other arithmetic, on_device(): jnp.sum(middle * middle, 0)  7.51 us
    slice x4, local copies, waits for them, and re-layouts, inner_laplacian(): jnp.roll(centre, -1, axis_num)  6.42 us
  transfers between devices with their start and end apart: 7, of which 4 were waited for; matrix products, arithmetic and copies ran while one was open for 7% of the time, Pallas kernels for 0%

profile of v1, /device:TPU:2, one launch (start us, length us, event | category | flops | bytes accessed | tf_op | source)
XLA Modules:
  0.0 277.8 jit_solution(11100177016406118229)
XLA Ops:
  6.5 2.4 multiply_reduce_fusion
  9.1 1.9 fusion.47
  11.8 5.7 %collective-permute-start = (f32[24,1,128,128]{3,2,1,0:T(8,128)}, f32[24,1,128,128]{3,2,1,0:T(8,128)S(1)}, u32[]{:S(2)}, u32[]{:S(2)}) collective-permute-start(f32[24,1,128,128]{3,2,1,0:T(8,128)} %get-tuple-element.22), channel_id=1, source_target_pairs={{8,0},{16,8},{24,16},{32,24},{40,32},{48,40},{56,48},{64,56},{72,6... | collective-permute-start | bytes 4718600 | tf_op jit(solution)/shard_map/ppermute | solution.py:19
  17.6 2.0 fusion.54
  19.6 2.2 fusion.55
  21.8 2.2 fusion.56
  24.1 20.9 %collective-permute-done = f32[24,1,128,128]{3,2,1,0:T(8,128)S(1)} collective-permute-done((f32[24,1,128,128]{3,2,1,0:T(8,128)}, f32[24,1,128,128]{3,2,1,0:T(8,128)S(1)}, u32[]{:S(2)}, u32[]{:S(2)}) %collective-permute-start) | collective-permute-done | bytes 1572896 | tf_op jit(solution)/shard_map/ppermute | solution.py:19
  45.0 23.9 %collective-permute-done.1 = f32[24,1,128,128]{3,2,1,0:T(8,128)} collective-permute-done((f32[24,1,128,128]{3,2,1,0:T(8,128)}, f32[24,1,128,128]{3,2,1,0:T(8,128)}, u32[]{:S(2)}, u32[]{:S(2)}) %collective-permute-start.1) | collective-permute-done | bytes 1572896 | tf_op jit(solution)/shard_map/ppermute | solution.py:16
  68.9 1.6 fusion
  70.5 2.3 fusion.44
  72.8 2.2 fusion.45
  75.0 2.3 fusion.46
  77.3 1.3 reduce_sum.46
  78.6 7.5 %multiply_reduce_fusion.3 = (f32[2,128,128]{2,1,0:T(8,128)}, f32[2,128,128]{2,1,0:T(8,128)}, f32[12,2,128,128]{3,2,1,0:T(8,128)}) fusion(f32[12,4,128,128]{3,2,1,0:T(8,128)} %copy-done.1, f32[12,2,128,128]{3,2,1,0:T(8,128)S(1)} %copy-done, f32[12,2,128,1]{3,2,1,0:T(8,128)} %get-tuple-element.40, f32[12,2,128,127]{3,2,1,0:T(8,128)} %get-tuple-element.42, ...), kind=kLoop, calls=%fused_computation.57 | loop fusion | flops 11337728 | bytes 17694816 | tf_op jit(solution)/shard_map/reduce_sum | solution.py:59
  86.2 1.0 fusion.43
  87.2 78.7 %all-reduce.6.cloned.1.call-done = (f32[2,128,128]{2,1,0:T(8,128)}, f32[2,128,128]{2,1,0:T(8,128)}) async-done(((f32[2,128,128]{2,1,0:T(8,128)}, f32[2,128,128]{2,1,0:T(8,128)}), (f32[2,128,128]{2,1,0:T(8,128)}, f32[2,128,128]{2,1,0:T(8,128)})) %all-reduce.6.cloned.1.call-update) | async-done | bytes 262160 | tf_op jit(solution)/shard_map/psum | solution.py:58
  166.0 1.0 broadcast_multiply_fusion.2
  167.0 8.8 %multiply_reduce_fusion.1 = (f32[2,128,128]{2,1,0:T(8,128)}, f32[12,2,128,128]{3,2,1,0:T(8,128)S(1)}, f32[12,2,128,128]{3,2,1,0:T(8,128)}) fusion(f32[12,2,128,128]{3,2,1,0:T(8,128)S(1)} %copy-done, f32[12]{0:T(128)S(1)} %copy-done.5, f32[12,2,128,128]{3,2,1,0:T(8,128)} %param.5, f32[12,2,128,1]{3,2,1,0:T(8,128)} %get-tuple-element.18, ...), kind=kLoop, calls=%fused_computation.55 | loop fusion | flops 10584064 | bytes 19267680 | tf_op jit(solution)/shard_map/reduce_sum | solution.py:69
  175.8 2.2 fusion.48
  178.0 2.2 fusion.49
  180.2 1.3 fusion.52
  182.0 2.0 fusion.50
  184.1 79.8 %all-reduce.4.cloned.1.call-done = f32[2,128,128]{2,1,0:T(8,128)} async-done(((f32[2,128,128]{2,1,0:T(8,128)}), f32[2,128,128]{2,1,0:T(8,128)}) %all-reduce.4.cloned.1.call-update) | async-done | bytes 131088 | tf_op jit(solution)/shard_map/psum | solution.py:69
  264.9 6.4 %fusion.20 = f32[12,2,128,128]{3,2,1,0:T(8,128)} fusion(f32[12,2,128,128]{3,2,1,0:T(8,128)} %get-tuple-element.11, f32[12,2,128,128]{3,2,1,0:T(8,128)S(1)} %get-tuple-element.10, f32[12,2,128,128]{3,2,1,0:T(8,128)S(1)} %copy-done, f32[12,1,128,128]{3,2,1,0:T(8,128)} %collective-permute-done.3, f32[12,1,128,128]{3,2,1,0:T(8,128)} %collective-permute-done.2, ...), kind=kLoop, calls=%fused_computation.29 | loop fusion | flops 10223616 | bytes 14417968 | tf_op jit(solution)/shard_map/sub | solution.py:70
  (31 shorter events, 2.5 us)
Async XLA Ops:
  6.5 2.4 copy-start.4
  6.5 70.8 %all-gather.3.cloned.1.call-start = ((), (), s32[]{:S(2)}) async-start(), calls=%async_computation.1 | async-start | bytes 1179648 | tf_op jit(solution)/shard_map/all_gather | solution.py:48
  9.1 2.7 copy-start.2
  9.1 8.5 %copy-start = (f32[12,2,128,128]{3,2,1,0:T(8,128)S(1)}, f32[12,2,128,128]{3,2,1,0:T(8,128)}, u32[]{:S(2)}) copy-start(f32[12,2,128,128]{3,2,1,0:T(8,128)} %param.4) | copy-start | bytes 4718596
  11.8 33.2 %collective-permute-start = (f32[24,1,128,128]{3,2,1,0:T(8,128)}, f32[24,1,128,128]{3,2,1,0:T(8,128)S(1)}, u32[]{:S(2)}, u32[]{:S(2)}) collective-permute-start(f32[24,1,128,128]{3,2,1,0:T(8,128)} %get-tuple-element.22), channel_id=1, source_target_pairs={{8,0},{16,8},{24,16},{32,24},{40,32},{48,40},{56,48},{64,56},{72,6... | collective-permute-start | bytes 4718600 | tf_op jit(solution)/shard_map/ppermute | solution.py:19
  17.5 51.4 %collective-permute-start.1 = (f32[24,1,128,128]{3,2,1,0:T(8,128)}, f32[24,1,128,128]{3,2,1,0:T(8,128)}, u32[]{:S(2)}, u32[]{:S(2)}) collective-permute-start(f32[24,1,128,128]{3,2,1,0:T(8,128)} %get-tuple-element.21), channel_id=1, source_target_pairs={{0,8},{8,16},{16,24},{24,32},{32,40},{40,48},{48,56},{56,64},{64,7... | collective-permute-start | bytes 4718600 | tf_op jit(solution)/shard_map/ppermute | solution.py:16
  17.5 148.5 %all-reduce.6.cloned.1.call-start = ((), (), s32[]{:S(2)}) async-start(), calls=%async_computation.2 | async-start | bytes 524288 | tf_op jit(solution)/shard_map/psum | solution.py:58
  21.8 47.0 %copy-start.3 = (f32[24,2,128,128]{3,2,1,0:T(8,128)S(1)}, f32[24,2,128,128]{3,2,1,0:T(8,128)}, u32[]{:S(2)}) copy-start(f32[24,2,128,128]{3,2,1,0:T(8,128)} %copy-done.2) | copy-start | bytes 9437188
  21.8 47.0 %copy-start.5 = (f32[12]{0:T(128)S(1)}, f32[12]{0:T(128)}, u32[]{:S(2)}) copy-start(f32[12]{0:T(128)} %param.6) | copy-start | bytes 148
  70.5 4.6 %copy-start.1 = (f32[12,4,128,128]{3,2,1,0:T(8,128)}, f32[12,4,128,128]{3,2,1,0:T(8,128)S(1)}, u32[]{:S(2)}) copy-start(f32[12,4,128,128]{3,2,1,0:T(8,128)S(1)} %fusion) | copy-start | bytes 9437188
  75.0 3.6 %copy-start.6 = (f32[12]{0:T(128)S(1)}, f32[12]{0:T(128)}, u32[]{:S(2)}) copy-start(f32[12]{0:T(128)} %param.7) | copy-start | bytes 148
  86.2 177.7 %all-reduce.4.cloned.1.call-start = ((), (), s32[]{:S(2)}) async-start(), calls=%async_computation | async-start | bytes 262144 | tf_op jit(solution)/shard_map/psum | solution.py:69
  181.5 83.3 %collective-permute-start.2 = (f32[12,1,128,128]{3,2,1,0:T(8,128)}, f32[12,1,128,128]{3,2,1,0:T(8,128)}, u32[]{:S(2)}, u32[]{:S(2)}) collective-permute-start(f32[12,1,128,128]{3,2,1,0:T(8,128)} %get-tuple-element.31), channel_id=1, source_target_pairs={{8,0},{16,8},{24,16},{32,24},{40,32},{48,40},{56,48},{64,56},{72,6... | collective-permute-start | bytes 2359304 | tf_op jit(solution)/shard_map/ppermute | solution.py:19
  181.5 83.4 %collective-permute-start.3 = (f32[12,1,128,128]{3,2,1,0:T(8,128)}, f32[12,1,128,128]{3,2,1,0:T(8,128)}, u32[]{:S(2)}, u32[]{:S(2)}) collective-permute-start(f32[12,1,128,128]{3,2,1,0:T(8,128)} %get-tuple-element.32), channel_id=1, source_target_pairs={{0,8},{8,16},{16,24},{24,32},{32,40},{40,48},{48,56},{56,64},{64,7... | collective-permute-start | bytes 2359304 | tf_op jit(solution)/shard_map/ppermute | solution.py:16
Sparse Core Ops, SparseCore 0:
  17.6 59.4 all-gather.2
  86.3 79.6 all-reduce.5
  182.1 81.7 all-reduce.3
